TPU v7x, 512 devices: a whole 4x4x16 slice. The times are simulated.
512 devices in a mesh: seq: 64 (over y, z), req: 8 (over x, core).
Axes of the slice: x: 4, y: 4, z: 16, core: 2. Of those that a mesh axis runs over, the one named last changes fastest.
Arguments:
- new_token_queries: bfloat16 [4, 64, 2048], P(None, 'req'), may hold values from -48 to 48
- new_token_keys: bfloat16 [4, 64, 1024], P(None, 'req'), may hold values from -48 to 48
- new_token_values: bfloat16 [4, 64, 1024], P(None, 'req'), may hold values from -6 to 6
- key_cache: bfloat16 [64, 2048, 1024], P('req', 'seq'), may hold values from -48 to 48
- value_cache: bfloat16 [64, 2048, 1024], P('req', 'seq'), may hold values from -6 to 6
- cache_len: int32 [64], P('req'), may hold values from 1 to 2048, 34816 in all
- resid: bfloat16 [4, 64, 2048], P(None, 'req'), may hold values from -6 to 6
- gain: bfloat16 [2048], replicated, may hold values from 0.5 to 1.5
- w_gate: bfloat16 [2048, 6144], P('seq', 'req'), may hold values from -0.125 to 0.125
- w_up: bfloat16 [2048, 6144], P('seq', 'req'), may hold values from -0.125 to 0.125
- w_down: bfloat16 [6144, 2048], P('req', 'seq'), may hold values from -0.078125 to 0.078125
Outputs:
- out: bfloat16 [4, 64, 2048], P(None, 'req')
All inputs are finite; a program needn't handle non-finite values. No bound on the sum of `cache_len` on one device may be relied on, other than what follows from the above.
Results may differ from a plain program's by a relative error of at most 0.006.
Values may be sent and summed in bfloat16 or wider, within the bound.
A program may use at most 128 MiB of HBM per device.

v0:
```python
import math
import jax
import jax.numpy as jnp
from jax import lax
from jax.sharding import PartitionSpec as P

QUERY_HEADS = 16
KEY_VALUE_HEADS = 8
HEAD_SIZE = 128
DECODE_STEPS = 4
NEG_FILL = -1e30
EPSILON = 1e-06


def page_partial(query_vector, key_row_set, value_row_set, valid):
    scores = jnp.einsum(
        "rkgd,rbkd->rkgb", query_vector, key_row_set, preferred_element_type=jnp.float32
    ) / math.sqrt(HEAD_SIZE)
    inside = valid[:, None, None, :]
    scores = jnp.where(inside, scores, NEG_FILL)
    highest = jnp.max(scores, axis=-1)
    weights = jnp.where(inside, jnp.exp(scores - highest[..., None]), 0.0).astype(jnp.bfloat16)
    totals = jnp.sum(weights.astype(jnp.float32), axis=-1)
    weighted = jnp.einsum(
        "rkgb,rbkd->rkgd", weights, value_row_set, preferred_element_type=jnp.float32
    )
    return (highest, totals, weighted)


def merge_pair(former, latter):
    highest = jnp.maximum(former[0], latter[0])
    first_scale = jnp.exp(former[0] - highest)
    second_scale = jnp.exp(latter[0] - highest)
    totals = first_scale * former[1] + second_scale * latter[1]
    weighted = first_scale[..., None] * former[2] + second_scale[..., None] * latter[2]
    return (highest, totals, weighted)


def body(
    new_token_queries,
    new_token_keys,
    new_token_values,
    key_cache,
    value_cache,
    cache_len,
    resid,
    gain,
    w_gate,
    w_up,
    w_down,
):
    count_of_rows = new_token_queries.shape[1]
    page_length = key_cache.shape[1]
    head_cluster = QUERY_HEADS // KEY_VALUE_HEADS
    slice_width = w_gate.shape[0]
    unit_count = w_gate.shape[1]
    seq_index = lax.axis_index("seq")
    positions = seq_index * page_length + jnp.arange(page_length, dtype=jnp.int32)
    valid = positions[None, :] < cache_len[:, None]
    key_row_set = key_cache.reshape(count_of_rows, page_length, KEY_VALUE_HEADS, HEAD_SIZE)
    value_row_set = value_cache.reshape(count_of_rows, page_length, KEY_VALUE_HEADS, HEAD_SIZE)
    joined = jnp.concatenate([w_gate, w_up], axis=1)
    gain_scale = gain.astype(jnp.float32)
    results = []
    for decode_step_index in range(DECODE_STEPS):
        query_vector = new_token_queries[decode_step_index].reshape(
            count_of_rows, KEY_VALUE_HEADS, head_cluster, HEAD_SIZE
        )
        local = page_partial(query_vector, key_row_set, value_row_set, valid)
        highest = lax.pmax(local[0], "seq")
        factor = jnp.exp(local[0] - highest)
        totals, weighted = lax.psum((factor * local[1], factor[..., None] * local[2]), "seq")
        incoming_keys = jnp.swapaxes(new_token_keys[: decode_step_index + 1], 0, 1).reshape(
            count_of_rows, decode_step_index + 1, KEY_VALUE_HEADS, HEAD_SIZE
        )
        incoming_values = jnp.swapaxes(new_token_values[: decode_step_index + 1], 0, 1).reshape(
            count_of_rows, decode_step_index + 1, KEY_VALUE_HEADS, HEAD_SIZE
        )
        fresh_valid = jnp.ones((count_of_rows, decode_step_index + 1), jnp.bool_)
        fresh = page_partial(query_vector, incoming_keys, incoming_values, fresh_valid)
        combined = merge_pair((highest, totals, weighted), fresh)
        attention = (
            (combined[2] / combined[1][..., None])
            .reshape(count_of_rows, QUERY_HEADS * HEAD_SIZE)
            .astype(jnp.bfloat16)
        )
        attention = lax.optimization_barrier(attention).astype(jnp.float32)
        stream = (resid[decode_step_index].astype(jnp.float32) + attention).astype(jnp.bfloat16)
        stream = lax.optimization_barrier(stream).astype(jnp.float32)
        scaled = lax.rsqrt(jnp.mean(stream * stream, axis=-1, keepdims=True) + EPSILON)
        normed = (stream * scaled * gain_scale).astype(jnp.bfloat16)
        own_slice = lax.dynamic_slice_in_dim(normed, seq_index * slice_width, slice_width, 1)
        partial_sums = jnp.dot(
            lax.all_gather(own_slice, "req", axis=0, tiled=True),
            joined,
            preferred_element_type=jnp.float32,
        )
        whole_sums = lax.psum(partial_sums, "seq")
        hidden = (jax.nn.silu(whole_sums[:, :unit_count]) * whole_sums[:, unit_count:]).astype(
            jnp.bfloat16
        )
        down_sum = lax.psum_scatter(
            jnp.dot(hidden, w_down, preferred_element_type=jnp.float32),
            "req",
            scatter_dimension=0,
            tiled=True,
        )
        stream_slice = lax.dynamic_slice_in_dim(stream, seq_index * slice_width, slice_width, 1)
        out_piece = (stream_slice + down_sum).astype(jnp.bfloat16)
        results.append(lax.all_gather(out_piece, "seq", axis=1, tiled=True))
    return jnp.stack(results)


def solution(mesh):
    placed = (
        P(None, "req", None),
        P(None, "req", None),
        P(None, "req", None),
        P("req", "seq", None),
        P("req", "seq", None),
        P("req"),
        P(None, "req", None),
        P(),
        P("seq", "req"),
        P("seq", "req"),
        P("req", "seq"),
    )
    return jax.shard_map(
        body, mesh=mesh, in_specs=placed, out_specs=P(None, "req", None), check_vma=False
    )
```

profile of v0, /device:TPU:8, one launch (start us, length us, event | category | flops | bytes accessed | tf_op | source)
XLA Modules:
  0.0 1327.7 jit_solution(7573360003918362906)
XLA Ops:
  6.5 0.9 fusion.88
  8.2 1.5 fusion.89
  11.1 261.7 %all-reduce.7 = (f32[8,8,2]{2,1,0:T(8,128)S(1)}, f32[8,8,2]{2,1,0:T(8,128)S(1)}, f32[8,8,2]{2,1,0:T(8,128)S(1)}, f32[8,8,2]{2,1,0:T(8,128)S(1)}) all-reduce(f32[8,8,2]{2,1,0:T(8,128)S(1)} %get-tuple-element.80, f32[8,8,2]{2,1,0:T(8,128)S(1)} %get-tuple-element.78, ...), channel_id=1, replica_groups=mesh['seq'=64,'req'=8] {'seq'}, use_global_device_ids=true, to_apply=%region_29.30 | all-reduce | flops 512 | bytes 4096 | tf_op jit(solution)/shard_map/pmax | solution.py:70
  273.5 0.9 convolution_multiply_fusion.11
  274.4 0.9 convolution_multiply_fusion.9
  275.3 0.9 convolution_multiply_fusion.7
  276.2 0.9 convolution_multiply_fusion.5
  280.1 274.1 %all-reduce.4 = (f32[8,8,2]{2,1,0:T(8,128)S(1)}, f32[8,8,2]{2,1,0:T(8,128)S(1)}, f32[8,8,2]{2,1,0:T(8,128)S(1)}, f32[8,8,2]{2,1,0:T(8,128)S(1)}) all-reduce(f32[8,8,2]{2,1,0:T(8,128)S(1)} %get-tuple-element.88, f32[8,8,2]{2,1,0:T(8,128)S(1)} %get-tuple-element.47, ...), channel_id=1, replica_groups=mesh['seq'=64,'req'=8] {'seq'}, use_global_device_ids=true, to_apply=%region_33.34 | all-reduce | flops 512 | bytes 4096 | tf_op jit(solution)/shard_map/psum | solution.py:72
  554.5 0.8 copy-done.6
  555.7 0.8 dynamic-slice.8
  556.6 1.2 fusion.11
  557.8 0.8 copy-done.13
  559.0 0.8 copy-done.12
  560.1 0.8 copy-done.4
  562.6 12.0 all_gather.24
  574.6 11.2 all_gather.26
  585.8 0.9 fusion.95
  586.8 0.9 fusion.96
  587.7 11.3 all_gather.28
  599.0 0.9 fusion.97
  599.9 11.2 all_gather.30
  611.2 0.9 fusion.98
  612.1 1.3 dynamic-slice
  614.0 286.2 %all-reduce.12.cloned.1.call-done = (f32[64,1536]{1,0:T(8,128)}, f32[64,1536]{1,0:T(8,128)}, f32[64,1536]{1,0:T(8,128)}, f32[64,1536]{1,0:T(8,128)}) async-done(((f32[64,1536]{1,0:T(8,128)}, f32[64,1536]{1,0:T(8,128)}, f32[64,1536]{1,0:T(8,128)}, f32[64,1536]{1,0:T(8,128)}), (f32[64,1536]{1,0:T(8,128)}, f32[64,1536]{1,0:T(8,128)}, f32[64,1536]{1,0:T(8,128)}, ...) | async-done | bytes 1572880 | tf_op jit(solution)/shard_map/psum | solution.py:98
  900.2 1.2 fusion.33
  901.7 0.8 copy-done.10
  902.7 0.8 copy-done.9
  903.7 24.8 %all-reduce.8 = (f32[64,32]{1,0:T(8,128)S(1)}, f32[64,32]{1,0:T(8,128)S(1)}, f32[64,32]{1,0:T(8,128)S(1)}, f32[64,32]{1,0:T(8,128)S(1)}) all-reduce(f32[64,32]{1,0:T(8,128)S(1)} %fusion.39, f32[64,32]{1,0:T(8,128)S(1)} %fusion.37, f32[64,32]{1,0:T(8,128)S(1)} %fusion.35, ...), channel_id=5, replica_groups=mesh['seq'=64,'req'=8] {'req'}, use_global_device_ids=true, to_apply=%region_37.38.clone | all-reduce | flops 8192 | bytes 65536
  928.6 97.9 %all-gather = bf16[64,32,8]{1,2,0:T(8,128)(2,1)S(1)} all-gather(bf16[1,32,8]{1,2,0:T(8,128)(2,1)S(1)} %fusion.68), channel_id=1, replica_groups=mesh['seq'=64,'req'=8] {'seq'}, dimensions={0}, use_global_device_ids=true | all-gather | bytes 33280 | tf_op jit(solution)/shard_map/all_gather | solution.py:110
  1026.8 97.5 %all-gather.1 = bf16[64,32,8]{1,2,0:T(8,128)(2,1)S(1)} all-gather(bf16[1,32,8]{1,2,0:T(8,128)(2,1)S(1)} %fusion.69), channel_id=1, replica_groups=mesh['seq'=64,'req'=8] {'seq'}, dimensions={0}, use_global_device_ids=true | all-gather | bytes 33280 | tf_op jit(solution)/shard_map/all_gather | solution.py:110
  1124.5 97.6 %all-gather.2 = bf16[64,32,8]{1,2,0:T(8,128)(2,1)S(1)} all-gather(bf16[1,32,8]{1,2,0:T(8,128)(2,1)S(1)} %fusion.70), channel_id=1, replica_groups=mesh['seq'=64,'req'=8] {'seq'}, dimensions={0}, use_global_device_ids=true | all-gather | bytes 33280 | tf_op jit(solution)/shard_map/all_gather | solution.py:110
  1222.5 97.5 %all-gather.3 = bf16[64,32,8]{1,2,0:T(8,128)(2,1)S(1)} all-gather(bf16[1,32,8]{1,2,0:T(8,128)(2,1)S(1)} %fusion.71), channel_id=1, replica_groups=mesh['seq'=64,'req'=8] {'seq'}, dimensions={0}, use_global_device_ids=true | all-gather | bytes 33280 | tf_op jit(solution)/shard_map/all_gather | solution.py:110
  (107 shorter events, 11.2 us)
Async XLA Ops:
  6.5 267.0 %copy-start = (bf16[8,32,1024]{2,1,0:T(8,128)(2,1)S(1)}, bf16[8,32,1024]{2,1,0:T(8,128)(2,1)}, u32[]{:S(2)}) copy-start(bf16[8,32,1024]{2,1,0:T(8,128)(2,1)} %param.15) | copy-start | bytes 1572868
  6.5 550.0 %all-reduce.14.cloned.1.call-start = ((), (), s32[]{:S(2)}) async-start(), calls=%async_computation.1 | async-start | bytes 524288 | tf_op jit(solution)/shard_map/psum | solution.py:72
  7.4 0.7 copy-start.7
  7.5 2.2 copy-start.8
  277.0 0.8 copy-start.1
  277.1 0.9 copy-start.2
  277.1 623.2 %all-reduce.12.cloned.1.call-start = ((), (), s32[]{:S(2)}) async-start(), calls=%async_computation | async-start | bytes 3145728 | tf_op jit(solution)/shard_map/psum | solution.py:98
  279.0 0.8 copy-start.5
  554.5 0.8 copy-start.6
  557.8 0.8 copy-start.13
  559.0 0.8 copy-start.12
  560.1 0.8 copy-start.4
  561.0 0.9 copy-start.3
  612.1 288.2 %copy-start.14 = (bf16[768,32]{0,1:T(8,128)(2,1)S(1)}, bf16[768,32]{0,1:T(8,128)(2,1)}, u32[]{:S(2)}) copy-start(bf16[768,32]{0,1:T(8,128)(2,1)} %param.21) | copy-start | bytes 147460
  900.2 1.3 copy-start.11
  901.5 1.0 copy-start.10
  902.5 1.0 copy-start.9
Sparse Core Ops, SparseCore 0:
  277.2 274.5 all-reduce.13
  612.2 287.9 all-reduce.11
where the time goes:
time: 1330 us
  blocking collectives  997 us (75%)
  waiting for transfers between devices  286 us (22%)
  matrix products  14.7 us (1%)
  between operations  14.5 us (1%)
    all_gather x4, blocking collectives, body(): results.append(lax.all_gather(out_piece, 'seq', axis=1, tiled=True))  391 us
    psum x1, waiting for transfers between devices, body(): whole_sums = lax.psum(partial_sums, 'seq')  286 us
    psum x1, blocking collectives, body(): lax.psum((factor * local[1], factor[..., None] * local[2]), 'seq')  274 us
    pmax x1, blocking collectives, body(): highest = lax.pmax(local[0], 'seq')  262 us
    all_gather x4, blocking collectives, body(): lax.all_gather(own_slice, 'req', axis=0, tiled=True)  45.8 us
  transfers between devices with their start and end apart: 2, of which 1 were waited for; matrix products, arithmetic and copies ran while one was open for 0% of the time, Pallas kernels for 0%

commit v1 on v0

--- a/solution.py
+++ b/solution.py
@@ -107,7 +107,11 @@
         )
         stream_slice = lax.dynamic_slice_in_dim(stream, seq_index * slice_width, slice_width, 1)
         out_piece = (stream_slice + down_sum).astype(jnp.bfloat16)
-        results.append(lax.all_gather(out_piece, "seq", axis=1, tiled=True))
+        results.append(
+            jnp.concatenate(
+                lax.all_to_all(jnp.stack([out_piece] * lax.axis_size("seq")), "seq", 0, 0), axis=1
+            )
+        )
     return jnp.stack(results)
 
 

time: 1330 us -> 1020 us (0.77)
  blocking collectives: 997 us -> 606 us
  waiting for transfers between devices: 286 us -> 337 us
  starting transfers between devices: 0.04 us -> 26.9 us
    all_gather x4 -> x0, blocking collectives: 391 us -> none  [body(): results.append(lax.all_gather(out_piece, 'seq', axis=1, tiled=True))]
    all_to_all x0 -> x4, waiting for transfers between devices: none -> 50.4 us  [body(): lax.all_to_all(jnp.stack([out_piece] * lax.axis_size('seq')), 'seq', 0, 0)]
    all_to_all x0 -> x4, starting transfers between devices: none -> 26.9 us  [body(): lax.all_to_all(jnp.stack([out_piece] * lax.axis_size('seq')), 'seq', 0, 0)]
  transfers between devices with their start and end apart: 2 -> 6, of which waited for: 1 -> 5; matrix products, arithmetic and copies ran while one was open for 0% -> 1% of each run, Pallas kernels for 0% -> 0%
where the time goes in v1:
time: 1020 us
  blocking collectives  606 us (59%)
  waiting for transfers between devices  337 us (33%)
  starting transfers between devices  26.9 us (3%)
  local copies, waits for them, and re-layouts  15.3 us (2%)
  matrix products  14.7 us (1%)
  between operations  14.6 us (1%)
    psum x1, waiting for transfers between devices, body(): whole_sums = lax.psum(partial_sums, 'seq')  286 us
    psum x1, blocking collectives, body(): lax.psum((factor * local[1], factor[..., None] * local[2]), 'seq')  274 us
    pmax x1, blocking collectives, body(): highest = lax.pmax(local[0], 'seq')  262 us
    all_to_all x4, waiting for transfers between devices, body(): lax.all_to_all(jnp.stack([out_piece] * lax.axis_size('seq')), 'seq', 0, 0)  50.4 us
    all_gather x4, blocking collectives, body(): lax.all_gather(own_slice, 'req', axis=0, tiled=True)  45.6 us
    all_to_all x4, starting transfers between devices, body(): lax.all_to_all(jnp.stack([out_piece] * lax.axis_size('seq')), 'seq', 0, 0)  26.9 us
    unnamed x1, blocking collectives  24.8 us
  transfers between devices with their start and end apart: 6, of which 5 were waited for; matrix products, arithmetic and copies ran while one was open for 1% of the time, Pallas kernels for 0%

profile of v1, /device:TPU:8, one launch (start us, length us, event | category | flops | bytes accessed | tf_op | source)
XLA Modules:
  0.0 1018.1 jit_solution(733708506438381974)
XLA Ops:
  6.5 0.9 fusion.84
  8.2 1.5 fusion.85
  11.1 261.7 %all-reduce.7 = (f32[8,8,2]{2,1,0:T(8,128)S(1)}, f32[8,8,2]{2,1,0:T(8,128)S(1)}, f32[8,8,2]{2,1,0:T(8,128)S(1)}, f32[8,8,2]{2,1,0:T(8,128)S(1)}) all-reduce(f32[8,8,2]{2,1,0:T(8,128)S(1)} %get-tuple-element.80, f32[8,8,2]{2,1,0:T(8,128)S(1)} %get-tuple-element.78, ...), channel_id=1, replica_groups=mesh['seq'=64,'req'=8] {'seq'}, use_global_device_ids=true, to_apply=%region_29.30 | all-reduce | flops 512 | bytes 4096 | tf_op jit(solution)/shard_map/pmax | solution.py:70
  273.5 0.9 convolution_multiply_fusion.11
  274.4 0.9 convolution_multiply_fusion.9
  275.3 0.9 convolution_multiply_fusion.7
  276.2 0.9 convolution_multiply_fusion.5
  280.1 274.2 %all-reduce.4 = (f32[8,8,2]{2,1,0:T(8,128)S(1)}, f32[8,8,2]{2,1,0:T(8,128)S(1)}, f32[8,8,2]{2,1,0:T(8,128)S(1)}, f32[8,8,2]{2,1,0:T(8,128)S(1)}) all-reduce(f32[8,8,2]{2,1,0:T(8,128)S(1)} %get-tuple-element.88, f32[8,8,2]{2,1,0:T(8,128)S(1)} %get-tuple-element.47, ...), channel_id=1, replica_groups=mesh['seq'=64,'req'=8] {'seq'}, use_global_device_ids=true, to_apply=%region_33.34 | all-reduce | flops 512 | bytes 4096 | tf_op jit(solution)/shard_map/psum | solution.py:72
  556.6 1.2 fusion.11
  559.1 0.8 copy-done.12
  560.2 0.8 copy-done.4
  562.7 11.9 %all_gather.12 = bf16[64,32]{1,0:T(8,128)(2,1)S(1)} all-gather(bf16[8,32]{1,0:T(8,128)(2,1)S(1)} %get-tuple-element.70), channel_id=1, replica_groups=mesh['seq'=64,'req'=8] {'req'}, dimensions={0}, use_global_device_ids=true | all-gather | bytes 4608 | tf_op jit(solution)/shard_map/all_gather | solution.py:94
  574.5 11.2 %all_gather.13 = bf16[64,32]{1,0:T(8,128)(2,1)S(1)} all-gather(bf16[8,32]{1,0:T(8,128)(2,1)S(1)} %get-tuple-element.71), channel_id=1, replica_groups=mesh['seq'=64,'req'=8] {'req'}, dimensions={0}, use_global_device_ids=true | all-gather | bytes 4608 | tf_op jit(solution)/shard_map/all_gather | solution.py:94
  585.7 0.9 fusion.91
  586.7 0.9 fusion.92
  587.6 11.3 %all_gather.14 = bf16[64,32]{1,0:T(8,128)(2,1)S(1)} all-gather(bf16[8,32]{1,0:T(8,128)(2,1)S(1)} %get-tuple-element.72), channel_id=1, replica_groups=mesh['seq'=64,'req'=8] {'req'}, dimensions={0}, use_global_device_ids=true | all-gather | bytes 4608 | tf_op jit(solution)/shard_map/all_gather | solution.py:94
  598.9 1.0 fusion.93
  599.9 11.2 %all_gather.15 = bf16[64,32]{1,0:T(8,128)(2,1)S(1)} all-gather(bf16[8,32]{1,0:T(8,128)(2,1)S(1)} %get-tuple-element.73), channel_id=1, replica_groups=mesh['seq'=64,'req'=8] {'req'}, dimensions={0}, use_global_device_ids=true | all-gather | bytes 4608 | tf_op jit(solution)/shard_map/all_gather | solution.py:94
  611.1 0.9 fusion.94
  612.0 1.3 dynamic-slice
  614.0 286.4 %all-reduce.12.cloned.1.call-done = (f32[64,1536]{1,0:T(8,128)}, f32[64,1536]{1,0:T(8,128)}, f32[64,1536]{1,0:T(8,128)}, f32[64,1536]{1,0:T(8,128)}) async-done(((f32[64,1536]{1,0:T(8,128)}, f32[64,1536]{1,0:T(8,128)}, f32[64,1536]{1,0:T(8,128)}, f32[64,1536]{1,0:T(8,128)}), (f32[64,1536]{1,0:T(8,128)}, f32[64,1536]{1,0:T(8,128)}, f32[64,1536]{1,0:T(8,128)}, ...) | async-done | bytes 1572880 | tf_op jit(solution)/shard_map/psum | solution.py:98
  900.3 1.2 fusion.33
  902.8 0.8 copy-done.9
  903.8 24.8 %all-reduce.8 = (f32[64,32]{1,0:T(8,128)S(1)}, f32[64,32]{1,0:T(8,128)S(1)}, f32[64,32]{1,0:T(8,128)S(1)}, f32[64,32]{1,0:T(8,128)S(1)}) all-reduce(f32[64,32]{1,0:T(8,128)S(1)} %fusion.39, f32[64,32]{1,0:T(8,128)S(1)} %fusion.37, f32[64,32]{1,0:T(8,128)S(1)} %fusion.35, ...), channel_id=5, replica_groups=mesh['seq'=64,'req'=8] {'req'}, use_global_device_ids=true, to_apply=%region_37.38.clone | all-reduce | flops 8192 | bytes 65536
  929.4 10.5 %all-to-all-start = ((bf16[64,2,128]{2,1,0:T(2,128)(2,1)}), bf16[64,2,128]{2,1,0:T(2,128)(2,1)S(1)}, u32[]{:S(2)}, u32[]{:S(2)}) async-start(bf16[64,2,128]{2,1,0:T(2,128)(2,1)} %reshape.203), calls=%async_computation | async-start | bytes 65536 | tf_op jit(solution)/shard_map/all_to_all | solution.py:112
  940.7 12.6 %all-to-all-done = bf16[64,2,128]{2,1,0:T(2,128)(2,1)S(1)} async-done(((bf16[64,2,128]{2,1,0:T(2,128)(2,1)}), bf16[64,2,128]{2,1,0:T(2,128)(2,1)S(1)}, u32[]{:S(2)}, u32[]{:S(2)}) %all-to-all-start) | async-done | bytes 32800 | tf_op jit(solution)/shard_map/all_to_all | solution.py:112
  953.4 5.5 all-to-all-start.1
  959.8 12.6 %all-to-all-done.1 = bf16[64,2,128]{2,1,0:T(2,128)(2,1)S(1)} async-done(((bf16[64,2,128]{2,1,0:T(2,128)(2,1)}), bf16[64,2,128]{2,1,0:T(2,128)(2,1)S(1)}, u32[]{:S(2)}, u32[]{:S(2)}) %all-to-all-start.1) | async-done | bytes 32800 | tf_op jit(solution)/shard_map/all_to_all | solution.py:112
  972.4 5.5 all-to-all-start.2
  978.8 12.7 %all-to-all-done.2 = bf16[64,2,128]{2,1,0:T(2,128)(2,1)S(1)} async-done(((bf16[64,2,128]{2,1,0:T(2,128)(2,1)}), bf16[64,2,128]{2,1,0:T(2,128)(2,1)S(1)}, u32[]{:S(2)}, u32[]{:S(2)}) %all-to-all-start.2) | async-done | bytes 32800 | tf_op jit(solution)/shard_map/all_to_all | solution.py:112
  991.4 5.4 all-to-all-start.3
  997.7 12.5 %all-to-all-done.3 = bf16[64,2,128]{2,1,0:T(2,128)(2,1)S(1)} async-done(((bf16[64,2,128]{2,1,0:T(2,128)(2,1)}), bf16[64,2,128]{2,1,0:T(2,128)(2,1)S(1)}, u32[]{:S(2)}, u32[]{:S(2)}) %all-to-all-start.3) | async-done | bytes 32800 | tf_op jit(solution)/shard_map/all_to_all | solution.py:112
  (123 shorter events, 17.8 us)
Async XLA Ops:
  6.5 267.0 %copy-start = (bf16[8,32,1024]{2,1,0:T(8,128)(2,1)S(1)}, bf16[8,32,1024]{2,1,0:T(8,128)(2,1)}, u32[]{:S(2)}) copy-start(bf16[8,32,1024]{2,1,0:T(8,128)(2,1)} %param.15) | copy-start | bytes 1572868
  6.5 550.1 %all-reduce.14.cloned.1.call-start = ((), (), s32[]{:S(2)}) async-start(), calls=%async_computation.5 | async-start | bytes 524288 | tf_op jit(solution)/shard_map/psum | solution.py:72
  7.4 0.7 copy-start.7
  7.5 2.2 copy-start.8
  277.0 0.8 copy-start.1
  277.1 0.9 copy-start.2
  277.1 623.2 %all-reduce.12.cloned.1.call-start = ((), (), s32[]{:S(2)}) async-start(), calls=%async_computation.4 | async-start | bytes 3145728 | tf_op jit(solution)/shard_map/psum | solution.py:98
  279.0 0.8 copy-start.5
  554.6 0.8 copy-start.6
  557.8 0.8 copy-start.13
  559.1 0.8 copy-start.12
  560.2 0.8 copy-start.4
  561.0 0.9 copy-start.3
  612.0 288.3 %copy-start.14 = (bf16[768,32]{0,1:T(8,128)(2,1)S(1)}, bf16[768,32]{0,1:T(8,128)(2,1)}, u32[]{:S(2)}) copy-start(bf16[768,32]{0,1:T(8,128)(2,1)} %param.21) | copy-start | bytes 147460
  900.3 1.3 copy-start.11
  901.6 1.0 copy-start.10
  902.6 1.0 copy-start.9
  929.4 24.0 %all-to-all-start = ((bf16[64,2,128]{2,1,0:T(2,128)(2,1)}), bf16[64,2,128]{2,1,0:T(2,128)(2,1)S(1)}, u32[]{:S(2)}, u32[]{:S(2)}) async-start(bf16[64,2,128]{2,1,0:T(2,128)(2,1)} %reshape.203), calls=%async_computation | async-start | bytes 65536 | tf_op jit(solution)/shard_map/all_to_all | solution.py:112
  953.4 19.0 %all-to-all-start.1 = ((bf16[64,2,128]{2,1,0:T(2,128)(2,1)}), bf16[64,2,128]{2,1,0:T(2,128)(2,1)S(1)}, u32[]{:S(2)}, u32[]{:S(2)}) async-start(bf16[64,2,128]{2,1,0:T(2,128)(2,1)} %reshape.201), calls=%async_computation.1 | async-start | bytes 65536 | tf_op jit(solution)/shard_map/all_to_all | solution.py:112
  972.4 19.0 %all-to-all-start.2 = ((bf16[64,2,128]{2,1,0:T(2,128)(2,1)}), bf16[64,2,128]{2,1,0:T(2,128)(2,1)S(1)}, u32[]{:S(2)}, u32[]{:S(2)}) async-start(bf16[64,2,128]{2,1,0:T(2,128)(2,1)} %reshape.199), calls=%async_computation.2 | async-start | bytes 65536 | tf_op jit(solution)/shard_map/all_to_all | solution.py:112
  991.4 18.8 %all-to-all-start.3 = ((bf16[64,2,128]{2,1,0:T(2,128)(2,1)}), bf16[64,2,128]{2,1,0:T(2,128)(2,1)S(1)}, u32[]{:S(2)}, u32[]{:S(2)}) async-start(bf16[64,2,128]{2,1,0:T(2,128)(2,1)} %reshape.197), calls=%async_computation.3 | async-start | bytes 65536 | tf_op jit(solution)/shard_map/all_to_all | solution.py:112
Sparse Core Ops, SparseCore 0:
  277.2 274.5 all-reduce.13
  612.2 288.1 all-reduce.11
